TPU v7x, 32 devices: a whole 2x2x4 slice. The times are simulated.
32 devices in a mesh: gx: 8 (over y, x, core), sp: 4 (over z).
Axes of the slice: x: 2, y: 2, z: 4, core: 2. Of those that a mesh axis runs over, the one named last changes fastest.
Arguments:
- previous_head: float32 [8, 64, 512], P(None, 'gx', 'sp'), may hold values from -6 to 6
- recharge: float32 [8, 64, 512], P(None, 'gx', 'sp'), may hold values from -6 to 6
- soil_zone: int32 [8, 64, 512], P(None, 'gx', 'sp'), may hold values from 0 to 7
- soil_cond: float32 [8], replicated, may hold values from 0.1 to 1
- soil_store: float32 [8], replicated, may hold values from 0.05 to 0.5
- species: float32 [12, 8, 64, 512], P('sp', None, 'gx'), may hold values from -6 to 6
- mineral_zone: int32 [8, 64, 512], P(None, 'gx', 'sp'), may hold values from 0 to 5
- rate_table: float32 [6, 8], replicated, may hold values from 0.3 to 3
- stoich: float32 [12, 8], replicated, may hold values from -3 to 3
- log_equil: float32 [8], replicated, may hold values from -1 to 1
Outputs:
- head_field: float32 [8, 64, 512], P(None, 'gx', 'sp')
- species_out: float32 [12, 8, 64, 512], P('sp', None, 'gx')
Inputs may be any that keep to these rules, and one draw needn't show every extreme that they name: `soil_zone`: a soil class of 8. `mineral_zone`: a mineral zone class of 6.
All inputs are finite; a program needn't handle non-finite values.
Results may differ from a plain program's by a relative error of at most 0.0003.
Values sent between devices are 32-bit elements; how exact they have to be, the bound alone decides.
No kernel may reach another device: no remote copies, remote signals or barrier semaphores. Data moves between devices by JAX's collectives and lax.ppermute only.
A program may use at most 64 MiB of HBM per device.

v0:
```python
import jax
import jax.numpy as jnp
from jax import lax
from jax.sharding import PartitionSpec as P

ITERS = 6
NEWTON = 2
time_step = 0.05
dispersion = 0.5
reaction_span = 0.5
newton_damping = 0.5


def padded_2(cells, sides, width):
    for axis, dim in sides:
        count = lax.axis_size(axis)
        ends = count - 1
        head = lax.slice_in_dim(cells, 0, width, axis=dim)
        tail = lax.slice_in_dim(cells, cells.shape[dim] - width, cells.shape[dim], axis=dim)
        cells = jnp.concatenate(
            [
                lax.ppermute(tail, axis, [(i, (i + 1) % count) for i in range(ends)]),
                cells,
                lax.ppermute(head, axis, [((i + 1) % count, i) for i in range(ends)]),
            ],
            axis=dim,
        )
    return cells


def harmonic(center, other):
    return 2.0 * center * other / (center + other)


def six_sides(padded):
    return [
        padded[..., 2:, 1:-1, 1:-1],
        padded[..., :-2, 1:-1, 1:-1],
        padded[..., 1:-1, 2:, 1:-1],
        padded[..., 1:-1, :-2, 1:-1],
        padded[..., 1:-1, 1:-1, 2:],
        padded[..., 1:-1, 1:-1, :-2],
    ]


def lookup(labels, entries):
    levels = jnp.arange(entries.shape[0], dtype=jnp.int32).reshape((-1,) + (1,) * labels.ndim)
    return jnp.sum(jnp.where(labels[None] == levels, entries.reshape(levels.shape), 0.0), axis=0)


def lookup_rows(labels, entries):
    levels = jnp.arange(entries.shape[0], dtype=jnp.int32)[:, None, None]
    return jnp.sum(jnp.where(labels[None, None, :] == levels, entries[:, :, None], 0.0), axis=0)


def transport(concentration, conc_padded, head_padded, cond_padded):
    head_center = head_padded[1:-1, 1:-1, 1:-1]
    conduct = cond_padded[1:-1, 1:-1, 1:-1]
    change = jnp.zeros_like(concentration)
    for beside, head_beside, cond_beside in zip(
        six_sides(conc_padded), six_sides(head_padded), six_sides(cond_padded)
    ):
        face_cond = harmonic(conduct, cond_beside)
        velocity = face_cond * (head_center - head_beside)
        change = (
            change
            + jnp.maximum(velocity, 0.0) * concentration
            + jnp.minimum(velocity, 0.0) * beside
        )
        change = change + dispersion * face_cond * (concentration - beside)
    return concentration - time_step * change


def solve_system(jacobian, mismatch):
    dimension = mismatch.shape[0]
    factor = [[None] * dimension for i in range(dimension)]
    inverse = [None] * dimension
    for j in range(dimension):
        for i in range(j, dimension):
            running = jacobian[i * dimension + j] + (1.0 if i == j else 0.0)
            for k in range(j):
                running = running - factor[i][k] * factor[j][k]
            if i == j:
                diag_root = jnp.sqrt(running)
                factor[j][j] = diag_root
                inverse[j] = 1.0 / diag_root
            else:
                factor[i][j] = running * inverse[j]
    forward = []
    for i in range(dimension):
        running = mismatch[i]
        for k in range(i):
            running = running - factor[i][k] * forward[k]
        forward.append(running * inverse[i])
    answer = [None] * dimension
    for i in reversed(range(dimension)):
        running = forward[i]
        for k in range(i + 1, dimension):
            running = running - factor[k][i] * answer[k]
        answer[i] = running * inverse[i]
    return jnp.stack(answer, 0)


def reaction(concentration, labels, rate_table, stoich, log_equil):
    rate_cells = lookup_rows(labels, rate_table)
    pair_products = (stoich[:, None, :] * stoich[None, :, :]).reshape(-1, stoich.shape[1])
    iterate = concentration
    for newton_pass in range(NEWTON):
        affinity = (
            jnp.dot(
                stoich.T,
                iterate,
                precision=lax.Precision.HIGHEST,
                preferred_element_type=jnp.float32,
            )
            - log_equil[:, None]
        )
        tangent = jnp.tanh(affinity)
        mismatch = (
            iterate
            - concentration
            + reaction_span
            * jnp.dot(
                stoich,
                rate_cells * tangent,
                precision=lax.Precision.HIGHEST,
                preferred_element_type=jnp.float32,
            )
        )
        jacobian = reaction_span * jnp.dot(
            pair_products,
            rate_cells * (1.0 - tangent * tangent),
            precision=lax.Precision.HIGHEST,
            preferred_element_type=jnp.float32,
        )
        iterate = iterate - newton_damping * solve_system(jacobian, mismatch)
    return iterate


def pad_vertical(field):
    return jnp.pad(field, ((1, 1), (0, 0), (0, 0)))


def to_cells(block):
    return lax.all_to_all(block, "sp", split_axis=3, concat_axis=0, tiled=True)


def per_device(
    previous_head,
    recharge,
    soil_zone,
    soil_cond,
    soil_store,
    species,
    mineral_zone,
    rate_table,
    stoich,
    log_equil,
):
    conduct = lookup(soil_zone, soil_cond)
    storage = lookup(soil_zone, soil_store)
    cond_padded = pad_vertical(padded_2(conduct, (("gx", 1), ("sp", 2)), 1))
    faces = [harmonic(conduct, beside) for beside in six_sides(cond_padded)]

    def operate(field):
        padded = pad_vertical(padded_2(field, (("gx", 1), ("sp", 2)), 1))
        result = storage * field
        for face_cond, beside in zip(faces, six_sides(padded)):
            result = result + face_cond * (field - beside)
        return result

    source = storage * previous_head + recharge
    head_field = jnp.zeros_like(source)
    residual = source

    def inner_pair(first, second):
        return lax.psum((jnp.sum(first * first), jnp.sum(first * second)), ("gx", "sp"))

    image = operate(residual)
    norm_now, product = inner_pair(residual, image)
    alpha = norm_now / product
    direction = residual
    along = image
    for iteration in range(ITERS):
        head_field = head_field + alpha * direction
        residual = residual - alpha * along
        if iteration + 1 < ITERS:
            image = operate(residual)
            norm_next, product = inner_pair(residual, image)
            ratio = norm_next / norm_now
            alpha = norm_next / (product - ratio * norm_next / alpha)
            direction = residual + ratio * direction
            along = image + ratio * along
            norm_now = norm_next
    head_rows, cond_rows = (
        lax.all_gather(head_field, "sp", axis=2, tiled=True),
        lax.all_gather(conduct, "sp", axis=2, tiled=True),
    )
    stacked = jnp.concatenate([species, head_rows[None], cond_rows[None]], 0)
    padded = padded_2(stacked, (("gx", 2),), 1)
    padded = jnp.pad(padded, ((0, 0), (1, 1), (0, 0), (1, 1)))
    moved = transport(species, padded[:-2], padded[-2], padded[-1])
    cells = to_cells(moved)
    block_shape = cells.shape
    reacted = reaction(
        cells.reshape(block_shape[0], -1), mineral_zone.reshape(-1), rate_table, stoich, log_equil
    )
    reacted = reacted.reshape(block_shape)
    species_out = lax.all_to_all(reacted, "sp", split_axis=0, concat_axis=3, tiled=True)
    return (head_field, species_out)


def solution(mesh):
    in_specs = (
        P(None, "gx", "sp"),
        P(None, "gx", "sp"),
        P(None, "gx", "sp"),
        P(),
        P(),
        P("sp", None, "gx", None),
        P(None, "gx", "sp"),
        P(),
        P(),
        P(),
    )
    out_specs = (P(None, "gx", "sp"), P("sp", None, "gx", None))
    return jax.shard_map(
        per_device, mesh=mesh, in_specs=in_specs, out_specs=out_specs, check_vma=False
    )
```

profile of v0, /device:TPU:2, one launch (start us, length us, event | category | flops | bytes accessed | tf_op | source)
XLA Modules:
  0.0 517.6 jit_solution(3128671705888314182)
XLA Ops:
  1.5 1.9 collective-permute-start.1
  3.5 2.4 collective-permute-start
  6.7 3.9 collective-permute-start.4
  10.5 1.9 collective-permute-start.5
  12.6 3.5 collective-permute-start.2
  18.8 5.2 %collective-permute-start.6 = (f32[8,10,1]{2,1,0:T(8,128)S(1)}, f32[8,10,1]{2,1,0:T(8,128)S(1)}, u32[]{:S(2)}, u32[]{:S(2)}) collective-permute-start(f32[8,10,1]{2,1,0:T(8,128)S(1)} %get-tuple-element.258), channel_id=1, source_target_pairs={{0,1},{1,2},{2,3},{4,5},{5,6},{6,7},{8,9},{9,10},{10,11},{12,13},{... | collective-permute-start | bytes 968 | tf_op jit(solution)/shard_map/ppermute | solution.py:22
  26.8 42.5 %all-reduce.13 = (f32[]{:T(128)}, f32[]{:T(128)}) all-reduce(f32[]{:T(128)} %get-tuple-element.13, f32[]{:T(128)} %get-tuple-element.12), channel_id=1, replica_groups=mesh['gx'=8,'sp'=4] {'gx','sp'}, use_global_device_ids=true, to_apply=%region_2.3 | all-reduce | flops 2 | bytes 16 | tf_op jit(solution)/shard_map/psum | solution.py:177
  70.7 1.9 collective-permute-start.8
  72.7 3.6 collective-permute-start.9
  79.0 4.5 collective-permute-start.10
  86.4 42.6 %all-reduce.12 = (f32[]{:T(128)}, f32[]{:T(128)}) all-reduce(f32[]{:T(128)} %get-tuple-element.11, f32[]{:T(128)} %get-tuple-element.10), channel_id=1, replica_groups=mesh['gx'=8,'sp'=4] {'gx','sp'}, use_global_device_ids=true, to_apply=%region_7.8 | all-reduce | flops 2 | bytes 16 | tf_op jit(solution)/shard_map/psum | solution.py:177
  133.6 1.9 collective-permute-start.12
  135.5 3.6 collective-permute-start.13
  142.0 4.5 collective-permute-start.14
  146.9 1.6 collective-permute-done.14
  149.3 42.4 %all-reduce.11 = (f32[]{:T(128)}, f32[]{:T(128)}) all-reduce(f32[]{:T(128)} %get-tuple-element.9, f32[]{:T(128)} %get-tuple-element.8), channel_id=1, replica_groups=mesh['gx'=8,'sp'=4] {'gx','sp'}, use_global_device_ids=true, to_apply=%region_11.12 | all-reduce | flops 2 | bytes 16 | tf_op jit(solution)/shard_map/psum | solution.py:177
  195.7 1.9 collective-permute-start.16
  197.6 3.6 collective-permute-start.17
  203.9 4.5 collective-permute-start.18
  211.3 42.3 %all-reduce.10 = (f32[]{:T(128)}, f32[]{:T(128)}) all-reduce(f32[]{:T(128)} %get-tuple-element.7, f32[]{:T(128)} %get-tuple-element.6), channel_id=1, replica_groups=mesh['gx'=8,'sp'=4] {'gx','sp'}, use_global_device_ids=true, to_apply=%region_15.16 | all-reduce | flops 2 | bytes 16 | tf_op jit(solution)/shard_map/psum | solution.py:177
  257.6 1.9 collective-permute-start.20
  259.5 3.6 collective-permute-start.21
  265.8 4.5 collective-permute-start.22
  273.2 42.3 %all-reduce.9 = (f32[]{:T(128)}, f32[]{:T(128)}) all-reduce(f32[]{:T(128)} %get-tuple-element.5, f32[]{:T(128)} %get-tuple-element.4), channel_id=1, replica_groups=mesh['gx'=8,'sp'=4] {'gx','sp'}, use_global_device_ids=true, to_apply=%region_19.20 | all-reduce | flops 2 | bytes 16 | tf_op jit(solution)/shard_map/psum | solution.py:177
  320.1 1.9 collective-permute-start.24
  322.0 3.6 collective-permute-start.25
  328.3 4.5 collective-permute-start.26
  332.9 13.5 %all_gather.7 = f32[8,8,512]{2,1,0:T(8,128)S(1)} all-gather(f32[8,8,128]{2,1,0:T(8,128)S(1)} %get-tuple-element.14), channel_id=1, replica_groups=mesh['gx'=8,'sp'=4] {'sp'}, dimensions={2}, use_global_device_ids=true | all-gather | bytes 163840 | tf_op jit(solution)/shard_map/all_gather | solution.py:197
  347.3 39.6 %all-reduce.8 = (f32[]{:T(128)}, f32[]{:T(128)}) all-reduce(f32[]{:T(128)} %get-tuple-element.210, f32[]{:T(128)} %fusion.320), channel_id=1, replica_groups=mesh['gx'=8,'sp'=4] {'gx','sp'}, use_global_device_ids=true, to_apply=%region_23.24 | all-reduce | flops 2 | bytes 16 | tf_op jit(solution)/shard_map/psum | solution.py:177
  390.8 13.5 %all_gather.6 = f32[8,8,512]{2,1,0:T(8,128)S(1)} all-gather(f32[8,8,128]{2,1,0:T(8,128)S(1)} %multiply_add_fusion), channel_id=1, replica_groups=mesh['gx'=8,'sp'=4] {'sp'}, dimensions={2}, use_global_device_ids=true | all-gather | bytes 163840 | tf_op jit(solution)/shard_map/all_gather | solution.py:196
  404.6 1.9 collective-permute-start.28
  406.5 14.5 %collective-permute-start.29 = (f32[5,8,1,512]{3,1,2,0:T(8,128)S(1)}, f32[5,8,1,512]{3,1,2,0:T(8,128)S(1)}, u32[]{:S(2)}, u32[]{:S(2)}) collective-permute-start(f32[5,8,1,512]{3,1,2,0:T(8,128)S(1)} %get-tuple-element.238), channel_id=1, source_target_pairs={{4,0},{8,4},{12,8},{16,12},{20,16},{24,20},{28,24},{5,1},{9,5},{13... | collective-permute-start | bytes 245768 | tf_op jit(solution)/shard_map/ppermute | solution.py:24
  424.1 4.1 copy.54
  428.2 6.1 %reshape.95 = f32[4,1,24576]{2,1,0:T(1,128)} reshape(f32[512,3,8,8]{3,2,1,0:T(8,128)} %bitcast.69) | data formatting | bytes 786432
  434.2 3.5 all-to-all-start
  438.2 11.8 %all-to-all-done = f32[4,1,24576]{2,1,0:T(1,128)S(1)} async-done(((f32[4,1,24576]{2,1,0:T(1,128)}), f32[4,1,24576]{2,1,0:T(1,128)S(1)}, u32[]{:S(2)}, u32[]{:S(2)}) %all-to-all-start) | async-done | bytes 393248 | tf_op jit(solution)/shard_map/all_to_all | solution.py:145
  450.5 1.8 reduce
  452.3 6.2 %reshape.96 = f32[512,3,8,8]{3,2,1,0:T(8,128)} reshape(f32[4,24576]{1,0:T(4,128)S(1)} %reduce) | data formatting | bytes 786432
  458.5 4.3 copy.55
  464.0 3.9 convolution_multiply_fusion.1
  467.9 7.2 %subtract_multiply_fusion.64 = (f32[1,8192]{1,0:T(1,128)S(1)}, f32[1,8192]{1,0:T(1,128)S(1)}, f32[1,8192]{1,0:T(1,128)S(1)}, f32[1,8192]{1,0:T(1,128)S(1)}, f32[...) fusion(f32[12,8192]{1,0:T(8,128)S(1)} %fusion.3, ...), kind=kLoop, calls=%fused_computation.862 | loop fusion | flops 5136384 | bytes 4751360 | tf_op jit(solution)/shard_map/mul | solution.py:94
  475.2 2.9 subtract_multiply_fusion.57
  478.1 4.1 subtract_multiply_fusion.46
  484.1 3.9 convolution_multiply_fusion
  488.0 7.3 %subtract_multiply_fusion.18 = (f32[1,8192]{1,0:T(1,128)S(1)}, f32[1,8192]{1,0:T(1,128)S(1)}, f32[1,8192]{1,0:T(1,128)S(1)}, f32[1,8192]{1,0:T(1,128)S(1)}, f32[...) fusion(f32[12,8192]{1,0:T(8,128)S(1)} %fusion.1, ...), kind=kLoop, calls=%fused_computation.808 | loop fusion | flops 5136384 | bytes 4751360 | tf_op jit(solution)/shard_map/mul | solution.py:94
  495.3 2.7 subtract_multiply_fusion.11
  498.0 4.1 subtract_multiply_fusion
  502.5 13.9 %all_to_all.33 = f32[12,8,8,128]{3,2,1,0:T(8,128)S(1)} all-to-all(f32[12,8,8,128]{3,2,1,0:T(8,128)S(1)} %fusion.11), channel_id=1, replica_groups=mesh['gx'=8,'sp'=4] {'sp'}, dimensions={0} | all-to-all | bytes 786432 | tf_op jit(solution)/shard_map/all_to_all | solution.py:209
  (137 shorter events, 40.2 us)
Async XLA Ops:
  1.5 11.0 %collective-permute-start.1 = (f32[8,1,128]{2,1,0:T(1,128)S(1)}, f32[8,1,128]{2,1,0:T(1,128)S(1)}, u32[]{:S(2)}, u32[]{:S(2)}) collective-permute-start(f32[8,1,128]{2,1,0:T(1,128)S(1)} %get-tuple-element.269), channel_id=1, source_target_pairs={{4,0},{8,4},{12,8},{16,12},{20,16},{24,20},{28,24},{5,1},{9,5},{13... | collective-permute-start | bytes 12296 | tf_op jit(solution)/shard_map/ppermute | solution.py:24
  3.5 9.0 %collective-permute-start = (f32[8,1,128]{2,1,0:T(1,128)S(1)}, f32[8,1,128]{2,1,0:T(1,128)S(1)}, u32[]{:S(2)}, u32[]{:S(2)}) collective-permute-start(f32[8,1,128]{2,1,0:T(1,128)S(1)} %get-tuple-element.270), channel_id=1, source_target_pairs={{0,4},{4,8},{8,12},{12,16},{16,20},{20,24},{24,28},{1,5},{5,9},{9,... | collective-permute-start | bytes 12296 | tf_op jit(solution)/shard_map/ppermute | solution.py:22
  6.7 10.7 %collective-permute-start.4 = (f32[8,1,128]{2,1,0:T(1,128)S(1)}, f32[8,1,128]{2,1,0:T(1,128)S(1)}, u32[]{:S(2)}, u32[]{:S(2)}) collective-permute-start(f32[8,1,128]{2,1,0:T(1,128)S(1)} %get-tuple-element.271), channel_id=1, source_target_pairs={{0,4},{4,8},{8,12},{12,16},{16,20},{20,24},{24,28},{1,5},{5,9},{9,... | collective-permute-start | bytes 12296 | tf_op jit(solution)/shard_map/ppermute | solution.py:22
  10.5 6.9 %collective-permute-start.5 = (f32[8,1,128]{2,1,0:T(1,128)S(1)}, f32[8,1,128]{2,1,0:T(1,128)S(1)}, u32[]{:S(2)}, u32[]{:S(2)}) collective-permute-start(f32[8,1,128]{2,1,0:T(1,128)S(1)} %get-tuple-element.272), channel_id=1, source_target_pairs={{4,0},{8,4},{12,8},{16,12},{20,16},{24,20},{28,24},{5,1},{9,5},{13... | collective-permute-start | bytes 12296 | tf_op jit(solution)/shard_map/ppermute | solution.py:24
  12.6 11.4 %collective-permute-start.2 = (f32[8,10,1]{2,1,0:T(8,128)S(1)}, f32[8,10,1]{2,1,0:T(8,128)S(1)}, u32[]{:S(2)}, u32[]{:S(2)}) collective-permute-start(f32[8,10,1]{2,1,0:T(8,128)S(1)} %get-tuple-element.255), channel_id=1, source_target_pairs={{0,1},{1,2},{2,3},{4,5},{5,6},{6,7},{8,9},{9,10},{10,11},{12,13},{... | collective-permute-start | bytes 968 | tf_op jit(solution)/shard_map/ppermute | solution.py:22
  16.1 7.9 %collective-permute-start.3 = (f32[8,10,1]{2,1,0:T(8,128)S(1)}, f32[8,10,1]{2,1,0:T(8,128)S(1)}, u32[]{:S(2)}, u32[]{:S(2)}) collective-permute-start(f32[8,10,1]{2,1,0:T(8,128)S(1)} %get-tuple-element.256), channel_id=1, source_target_pairs={{1,0},{2,1},{3,2},{5,4},{6,5},{7,6},{9,8},{10,9},{11,10},{13,12},{... | collective-permute-start | bytes 968 | tf_op jit(solution)/shard_map/ppermute | solution.py:24
  17.5 6.8 %collective-permute-start.7 = (f32[8,10,1]{2,1,0:T(8,128)S(1)}, f32[8,10,1]{2,1,0:T(8,128)S(1)}, u32[]{:S(2)}, u32[]{:S(2)}) collective-permute-start(f32[8,10,1]{2,1,0:T(8,128)S(1)} %get-tuple-element.257), channel_id=1, source_target_pairs={{1,0},{2,1},{3,2},{5,4},{6,5},{7,6},{9,8},{10,9},{11,10},{13,12},{... | collective-permute-start | bytes 968 | tf_op jit(solution)/shard_map/ppermute | solution.py:24
  18.8 7.1 %collective-permute-start.6 = (f32[8,10,1]{2,1,0:T(8,128)S(1)}, f32[8,10,1]{2,1,0:T(8,128)S(1)}, u32[]{:S(2)}, u32[]{:S(2)}) collective-permute-start(f32[8,10,1]{2,1,0:T(8,128)S(1)} %get-tuple-element.258), channel_id=1, source_target_pairs={{0,1},{1,2},{2,3},{4,5},{5,6},{6,7},{8,9},{9,10},{10,11},{12,13},{... | collective-permute-start | bytes 968 | tf_op jit(solution)/shard_map/ppermute | solution.py:22
  70.7 5.6 %collective-permute-start.8 = (f32[8,1,128]{2,1,0:T(1,128)S(1)}, f32[8,1,128]{2,1,0:T(1,128)S(1)}, u32[]{:S(2)}, u32[]{:S(2)}) collective-permute-start(f32[8,1,128]{2,1,0:T(1,128)S(1)} %get-tuple-element.267), channel_id=1, source_target_pairs={{0,4},{4,8},{8,12},{12,16},{16,20},{20,24},{24,28},{1,5},{5,9},{9,... | collective-permute-start | bytes 12296 | tf_op jit(solution)/shard_map/ppermute | solution.py:22
  72.7 5.0 collective-permute-start.9
  77.7 6.2 %collective-permute-start.11 = (f32[8,10,1]{2,1,0:T(8,128)S(1)}, f32[8,10,1]{2,1,0:T(8,128)S(1)}, u32[]{:S(2)}, u32[]{:S(2)}) collective-permute-start(f32[8,10,1]{2,1,0:T(8,128)S(1)} %get-tuple-element.253), channel_id=1, source_target_pairs={{1,0},{2,1},{3,2},{5,4},{6,5},{7,6},{9,8},{10,9},{11,10},{13,12},{... | collective-permute-start | bytes 968 | tf_op jit(solution)/shard_map/ppermute | solution.py:24
  79.0 6.4 %collective-permute-start.10 = (f32[8,10,1]{2,1,0:T(8,128)S(1)}, f32[8,10,1]{2,1,0:T(8,128)S(1)}, u32[]{:S(2)}, u32[]{:S(2)}) collective-permute-start(f32[8,10,1]{2,1,0:T(8,128)S(1)} %get-tuple-element.254), channel_id=1, source_target_pairs={{0,1},{1,2},{2,3},{4,5},{5,6},{6,7},{8,9},{9,10},{10,11},{12,13},{... | collective-permute-start | bytes 968 | tf_op jit(solution)/shard_map/ppermute | solution.py:22
  133.6 5.6 %collective-permute-start.12 = (f32[8,1,128]{2,1,0:T(1,128)S(1)}, f32[8,1,128]{2,1,0:T(1,128)S(1)}, u32[]{:S(2)}, u32[]{:S(2)}) collective-permute-start(f32[8,1,128]{2,1,0:T(1,128)S(1)} %get-tuple-element.265), channel_id=1, source_target_pairs={{0,4},{4,8},{8,12},{12,16},{16,20},{20,24},{24,28},{1,5},{5,9},{9,... | collective-permute-start | bytes 12296 | tf_op jit(solution)/shard_map/ppermute | solution.py:22
  135.5 5.0 collective-permute-start.13
  140.5 185.2 %copy-start = (f32[3,8,8,512]{3,2,1,0:T(8,128)S(1)}, f32[3,8,8,512]{3,2,1,0:T(8,128)}, u32[]{:S(2)}) copy-start(f32[3,8,8,512]{3,2,1,0:T(8,128)} %param.15) | copy-start | bytes 1179652
  140.6 6.3 %collective-permute-start.15 = (f32[8,10,1]{2,1,0:T(8,128)S(1)}, f32[8,10,1]{2,1,0:T(8,128)S(1)}, u32[]{:S(2)}, u32[]{:S(2)}) collective-permute-start(f32[8,10,1]{2,1,0:T(8,128)S(1)} %get-tuple-element.251), channel_id=1, source_target_pairs={{1,0},{2,1},{3,2},{5,4},{6,5},{7,6},{9,8},{10,9},{11,10},{13,12},{... | collective-permute-start | bytes 968 | tf_op jit(solution)/shard_map/ppermute | solution.py:24
  142.0 6.4 %collective-permute-start.14 = (f32[8,10,1]{2,1,0:T(8,128)S(1)}, f32[8,10,1]{2,1,0:T(8,128)S(1)}, u32[]{:S(2)}, u32[]{:S(2)}) collective-permute-start(f32[8,10,1]{2,1,0:T(8,128)S(1)} %get-tuple-element.252), channel_id=1, source_target_pairs={{0,1},{1,2},{2,3},{4,5},{5,6},{6,7},{8,9},{9,10},{10,11},{12,13},{... | collective-permute-start | bytes 968 | tf_op jit(solution)/shard_map/ppermute | solution.py:22
  195.7 5.6 %collective-permute-start.16 = (f32[8,1,128]{2,1,0:T(1,128)S(1)}, f32[8,1,128]{2,1,0:T(1,128)S(1)}, u32[]{:S(2)}, u32[]{:S(2)}) collective-permute-start(f32[8,1,128]{2,1,0:T(1,128)S(1)} %get-tuple-element.263), channel_id=1, source_target_pairs={{0,4},{4,8},{8,12},{12,16},{16,20},{20,24},{24,28},{1,5},{5,9},{9,... | collective-permute-start | bytes 12296 | tf_op jit(solution)/shard_map/ppermute | solution.py:22
  197.6 5.0 collective-permute-start.17
  202.7 6.2 %collective-permute-start.19 = (f32[8,10,1]{2,1,0:T(8,128)S(1)}, f32[8,10,1]{2,1,0:T(8,128)S(1)}, u32[]{:S(2)}, u32[]{:S(2)}) collective-permute-start(f32[8,10,1]{2,1,0:T(8,128)S(1)} %get-tuple-element.249), channel_id=1, source_target_pairs={{1,0},{2,1},{3,2},{5,4},{6,5},{7,6},{9,8},{10,9},{11,10},{13,12},{... | collective-permute-start | bytes 968 | tf_op jit(solution)/shard_map/ppermute | solution.py:24
  203.9 6.4 %collective-permute-start.18 = (f32[8,10,1]{2,1,0:T(8,128)S(1)}, f32[8,10,1]{2,1,0:T(8,128)S(1)}, u32[]{:S(2)}, u32[]{:S(2)}) collective-permute-start(f32[8,10,1]{2,1,0:T(8,128)S(1)} %get-tuple-element.250), channel_id=1, source_target_pairs={{0,1},{1,2},{2,3},{4,5},{5,6},{6,7},{8,9},{9,10},{10,11},{12,13},{... | collective-permute-start | bytes 968 | tf_op jit(solution)/shard_map/ppermute | solution.py:22
  257.6 5.6 %collective-permute-start.20 = (f32[8,1,128]{2,1,0:T(1,128)S(1)}, f32[8,1,128]{2,1,0:T(1,128)S(1)}, u32[]{:S(2)}, u32[]{:S(2)}) collective-permute-start(f32[8,1,128]{2,1,0:T(1,128)S(1)} %get-tuple-element.261), channel_id=1, source_target_pairs={{0,4},{4,8},{8,12},{12,16},{16,20},{20,24},{24,28},{1,5},{5,9},{9,... | collective-permute-start | bytes 12296 | tf_op jit(solution)/shard_map/ppermute | solution.py:22
  259.5 5.0 collective-permute-start.21
  264.5 6.2 %collective-permute-start.23 = (f32[8,10,1]{2,1,0:T(8,128)S(1)}, f32[8,10,1]{2,1,0:T(8,128)S(1)}, u32[]{:S(2)}, u32[]{:S(2)}) collective-permute-start(f32[8,10,1]{2,1,0:T(8,128)S(1)} %get-tuple-element.247), channel_id=1, source_target_pairs={{1,0},{2,1},{3,2},{5,4},{6,5},{7,6},{9,8},{10,9},{11,10},{13,12},{... | collective-permute-start | bytes 968 | tf_op jit(solution)/shard_map/ppermute | solution.py:24
  265.8 6.4 %collective-permute-start.22 = (f32[8,10,1]{2,1,0:T(8,128)S(1)}, f32[8,10,1]{2,1,0:T(8,128)S(1)}, u32[]{:S(2)}, u32[]{:S(2)}) collective-permute-start(f32[8,10,1]{2,1,0:T(8,128)S(1)} %get-tuple-element.248), channel_id=1, source_target_pairs={{0,1},{1,2},{2,3},{4,5},{5,6},{6,7},{8,9},{9,10},{10,11},{12,13},{... | collective-permute-start | bytes 968 | tf_op jit(solution)/shard_map/ppermute | solution.py:22
  320.1 5.8 %collective-permute-start.24 = (f32[8,1,128]{2,1,0:T(1,128)S(1)}, f32[8,1,128]{2,1,0:T(1,128)S(1)}, u32[]{:S(2)}, u32[]{:S(2)}) collective-permute-start(f32[8,1,128]{2,1,0:T(1,128)S(1)} %get-tuple-element.259), channel_id=1, source_target_pairs={{0,4},{4,8},{8,12},{12,16},{16,20},{20,24},{24,28},{1,5},{5,9},{9,... | collective-permute-start | bytes 12296 | tf_op jit(solution)/shard_map/ppermute | solution.py:22
  322.0 5.0 collective-permute-start.25
  327.1 19.3 %collective-permute-start.27 = (f32[8,10,1]{2,1,0:T(8,128)S(1)}, f32[8,10,1]{2,1,0:T(8,128)S(1)}, u32[]{:S(2)}, u32[]{:S(2)}) collective-permute-start(f32[8,10,1]{2,1,0:T(8,128)S(1)} %get-tuple-element.245), channel_id=1, source_target_pairs={{1,0},{2,1},{3,2},{5,4},{6,5},{7,6},{9,8},{10,9},{11,10},{13,12},{... | collective-permute-start | bytes 968 | tf_op jit(solution)/shard_map/ppermute | solution.py:24
  328.3 18.0 %collective-permute-start.26 = (f32[8,10,1]{2,1,0:T(8,128)S(1)}, f32[8,10,1]{2,1,0:T(8,128)S(1)}, u32[]{:S(2)}, u32[]{:S(2)}) collective-permute-start(f32[8,10,1]{2,1,0:T(8,128)S(1)} %get-tuple-element.246), channel_id=1, source_target_pairs={{0,1},{1,2},{2,3},{4,5},{5,6},{6,7},{8,9},{9,10},{10,11},{12,13},{... | collective-permute-start | bytes 968 | tf_op jit(solution)/shard_map/ppermute | solution.py:22
  390.8 30.9 %copy-start.2 = (f32[8,8,128]{2,1,0:T(8,128)}, f32[8,8,128]{2,1,0:T(8,128)S(1)}, u32[]{:S(2)}) copy-start(f32[8,8,128]{2,1,0:T(8,128)S(1)} %multiply_add_fusion) | copy-start | bytes 98308
  404.6 16.4 %collective-permute-start.28 = (f32[5,8,1,512]{3,1,2,0:T(8,128)S(1)}, f32[5,8,1,512]{3,1,2,0:T(8,128)S(1)}, u32[]{:S(2)}, u32[]{:S(2)}) collective-permute-start(f32[5,8,1,512]{3,1,2,0:T(8,128)S(1)} %get-tuple-element.237), channel_id=1, source_target_pairs={{0,4},{4,8},{8,12},{12,16},{16,20},{20,24},{24,28},{1,5},{5,9},{9,... | collective-permute-start | bytes 245768 | tf_op jit(solution)/shard_map/ppermute | solution.py:22
  406.5 14.5 %collective-permute-start.29 = (f32[5,8,1,512]{3,1,2,0:T(8,128)S(1)}, f32[5,8,1,512]{3,1,2,0:T(8,128)S(1)}, u32[]{:S(2)}, u32[]{:S(2)}) collective-permute-start(f32[5,8,1,512]{3,1,2,0:T(8,128)S(1)} %get-tuple-element.238), channel_id=1, source_target_pairs={{4,0},{8,4},{12,8},{16,12},{20,16},{24,20},{28,24},{5,1},{9,5},{13... | collective-permute-start | bytes 245768 | tf_op jit(solution)/shard_map/ppermute | solution.py:24
  428.2 9.5 %copy-start.3 = (s32[8,8,128]{2,1,0:T(8,128)S(1)}, s32[8,8,128]{2,1,0:T(8,128)}, u32[]{:S(2)}) copy-start(s32[8,8,128]{2,1,0:T(8,128)} %param.16) | copy-start | bytes 98308
  428.2 9.6 %copy-start.1 = (f32[12,8]{0,1:T(8,128)S(1)}, f32[12,8]{0,1:T(8,128)}, u32[]{:S(2)}) copy-start(f32[12,8]{0,1:T(8,128)} %param.18) | copy-start | bytes 1156
  428.2 9.8 %copy-start.4 = (f32[6,8]{1,0:T(8,128)S(1)}, f32[6,8]{1,0:T(8,128)}, u32[]{:S(2)}) copy-start(f32[6,8]{1,0:T(8,128)} %param.17) | copy-start | bytes 580
  434.2 15.8 %all-to-all-start = ((f32[4,1,24576]{2,1,0:T(1,128)}), f32[4,1,24576]{2,1,0:T(1,128)S(1)}, u32[]{:S(2)}, u32[]{:S(2)}) async-start(f32[4,1,24576]{2,1,0:T(1,128)} %reshape.95), calls=%async_computation | async-start | bytes 786432 | tf_op jit(solution)/shard_map/all_to_all | solution.py:145
  458.5 4.4 copy-start.5
where the time goes:
time: 527 us; the launch traced here: 518 us
  blocking collectives  293 us (56%)
  starting transfers between devices  98.3 us (19%)
  other arithmetic  41.7 us (8%)
  waiting for transfers between devices  27.3 us (5%)
  local copies, waits for them, and re-layouts  24 us (5%)
  between operations  23.5 us (4%)
  matrix products  10.1 us (2%)
    psum x6, blocking collectives, inner_pair(): lax.psum((jnp.sum(first * first), jnp.sum(first * second)), ('gx', 'sp'))  252 us
    ppermute x15, starting transfers between devices, padded_2(): lax.ppermute(tail, axis, [(i, (i + 1) % count) for i in range(ends)])  49.2 us
    ppermute x15, starting transfers between devices, padded_2(): lax.ppermute(head, axis, [((i + 1) % count, i) for i in range(ends)])  45.7 us
    mul x2, other arithmetic, solve_system(): forward.append(running * inverse[i])  14.5 us
    all_to_all x1, blocking collectives, per_device(): lax.all_to_all(reacted, 'sp', split_axis=0, concat_axis=3, tiled=True)  13.9 us
    all_gather x1, blocking collectives, per_device(): lax.all_gather(head_field, 'sp', axis=2, tiled=True)  13.5 us
    all_gather x1, blocking collectives, per_device(): lax.all_gather(conduct, 'sp', axis=2, tiled=True)  13.5 us
    unnamed x38, local copies, waits for them, and re-layouts  12.7 us
  transfers between devices with their start and end apart: 31, of which 16 were waited for; matrix products, arithmetic and copies ran while one was open for 0% of the time, Pallas kernels for 0%

commit v1 on v0

--- a/solution.py
+++ b/solution.py
@@ -1,7 +1,9 @@
+import functools
 import jax
 import jax.numpy as jnp
 from jax import lax
 from jax.sharding import PartitionSpec as P
+from jax.lax import psum
 
 ITERS = 6
 NEWTON = 2
@@ -9,6 +11,14 @@
 dispersion = 0.5
 reaction_span = 0.5
 newton_damping = 0.5
+
+
+def finish_scenes(t0, along_axis, dev_axis):
+    later = psum(psum(t0, along_axis), dev_axis)
+    return later
+
+
+_open_slabs = functools.partial(finish_scenes, along_axis="gx", dev_axis="sp")
 
 
 def padded_2(cells, sides, width):
@@ -174,7 +184,7 @@
     residual = source
 
     def inner_pair(first, second):
-        return lax.psum((jnp.sum(first * first), jnp.sum(first * second)), ("gx", "sp"))
+        return _open_slabs((jnp.sum(first * first), jnp.sum(first * second)))
 
     image = operate(residual)
     norm_now, product = inner_pair(residual, image)

time: 527 us -> 411 us (0.78); the launches traced: 518 us -> 409 us
  blocking collectives: 293 us -> 187 us
  starting transfers between devices: 98.3 us -> 87.7 us
  waiting for transfers between devices: 27.3 us -> 35.8 us
    psum x6 -> x12, blocking collectives: 252 us -> 143 us  [finish_scenes(): later = psum(psum(t0, along_axis), dev_axis)]
    ppermute x15, starting transfers between devices: 45.7 us -> 34.8 us  [padded_2(): lax.ppermute(head, axis, [((i + 1) % count, i) for i in range(ends)])]
    ppermute x15, waiting for transfers between devices: 7.58 us -> 18.3 us  [padded_2(): lax.ppermute(head, axis, [((i + 1) % count, i) for i in range(ends)])]
  transfers between devices with their start and end apart: 31 -> 31, of which waited for: 16 -> 18; matrix products, arithmetic and copies ran while one was open for 0% -> 0% of each run, Pallas kernels for 0% -> 0%
where the time goes in v1:
time: 411 us; the launch traced here: 409 us
  blocking collectives  187 us (45%)
  starting transfers between devices  87.7 us (21%)
  other arithmetic  41.9 us (10%)
  waiting for transfers between devices  35.8 us (9%)
  local copies, waits for them, and re-layouts  24 us (6%)
  between operations  23.1 us (6%)
  matrix products  10.1 us (2%)
    psum x12, blocking collectives, finish_scenes(): later = psum(psum(t0, along_axis), dev_axis)  143 us
    ppermute x15, starting transfers between devices, padded_2(): lax.ppermute(tail, axis, [(i, (i + 1) % count) for i in range(ends)])  49.2 us
    ppermute x15, starting transfers between devices, padded_2(): lax.ppermute(head, axis, [((i + 1) % count, i) for i in range(ends)])  34.8 us
    ppermute x15, waiting for transfers between devices, padded_2(): lax.ppermute(head, axis, [((i + 1) % count, i) for i in range(ends)])  18.3 us
    all_to_all x1, blocking collectives, per_device(): lax.all_to_all(reacted, 'sp', split_axis=0, concat_axis=3, tiled=True)  17.4 us
    mul x2, other arithmetic, solve_system(): forward.append(running * inverse[i])  14.5 us
    all_gather x1, blocking collectives, per_device(): lax.all_gather(conduct, 'sp', axis=2, tiled=True)  13.6 us
    all_gather x1, blocking collectives, per_device(): lax.all_gather(head_field, 'sp', axis=2, tiled=True)  13.4 us
  transfers between devices with their start and end apart: 31, of which 18 were waited for; matrix products, arithmetic and copies ran while one was open for 0% of the time, Pallas kernels for 0%

profile of v1, /device:TPU:2, one launch (start us, length us, event | category | flops | bytes accessed | tf_op | source)
XLA Modules:
  0.0 409.5 jit_solution(17676106246976844474)
XLA Ops:
  6.7 3.9 collective-permute-start.4
  12.6 3.5 collective-permute-start.2
  18.8 5.2 %collective-permute-start.6 = (f32[8,10,1]{2,1,0:T(8,128)S(1)}, f32[8,10,1]{2,1,0:T(8,128)S(1)}, u32[]{:S(2)}, u32[]{:S(2)}) collective-permute-start(f32[8,10,1]{2,1,0:T(8,128)S(1)} %get-tuple-element.270), channel_id=1, source_target_pairs={{0,1},{1,2},{2,3},{4,5},{5,6},{6,7},{8,9},{9,10},{10,11},{12,13},{... | collective-permute-start | bytes 968 | tf_op jit(solution)/shard_map/ppermute | solution.py:32
  26.8 11.3 %all-reduce.13 = (f32[]{:T(128)}, f32[]{:T(128)}) all-reduce(f32[]{:T(128)} %get-tuple-element.13, f32[]{:T(128)} %get-tuple-element.12), channel_id=1, replica_groups=mesh['gx'=8,'sp'=4] {'gx'}, use_global_device_ids=true, to_apply=%region_2.3 | all-reduce | flops 2 | bytes 16 | tf_op jit(solution)/shard_map/psum | solution.py:17
  38.2 13.8 %all-reduce.19 = (f32[]{:T(128)}, f32[]{:T(128)}) all-reduce(f32[]{:T(128)} %get-tuple-element.26, f32[]{:T(128)} %get-tuple-element.27), channel_id=1, replica_groups=mesh['gx'=8,'sp'=4] {'sp'}, use_global_device_ids=true, to_apply=%region_3.4 | all-reduce | flops 2 | bytes 16 | tf_op jit(solution)/shard_map/psum | solution.py:17
  55.3 3.6 collective-permute-start.9
  58.9 2.7 collective-permute-done.9
  63.0 4.5 %collective-permute-start.10 = (f32[8,10,1]{2,1,0:T(8,128)S(1)}, f32[8,10,1]{2,1,0:T(8,128)S(1)}, u32[]{:S(2)}, u32[]{:S(2)}) collective-permute-start(f32[8,10,1]{2,1,0:T(8,128)S(1)} %get-tuple-element.266), channel_id=1, source_target_pairs={{0,1},{1,2},{2,3},{4,5},{5,6},{6,7},{8,9},{9,10},{10,11},{12,13},{... | collective-permute-start | bytes 968 | tf_op jit(solution)/shard_map/ppermute | solution.py:32
  70.4 13.1 %all-reduce.12 = (f32[]{:T(128)}, f32[]{:T(128)}) all-reduce(f32[]{:T(128)} %get-tuple-element.11, f32[]{:T(128)} %get-tuple-element.10), channel_id=1, replica_groups=mesh['gx'=8,'sp'=4] {'gx'}, use_global_device_ids=true, to_apply=%region_9.10 | all-reduce | flops 2 | bytes 16 | tf_op jit(solution)/shard_map/psum | solution.py:17
  83.4 11.1 %all-reduce.18 = (f32[]{:T(128)}, f32[]{:T(128)}) all-reduce(f32[]{:T(128)} %get-tuple-element.24, f32[]{:T(128)} %get-tuple-element.25), channel_id=1, replica_groups=mesh['gx'=8,'sp'=4] {'sp'}, use_global_device_ids=true, to_apply=%region_10.11 | all-reduce | flops 2 | bytes 16 | tf_op jit(solution)/shard_map/psum | solution.py:17
  101.0 3.6 collective-permute-start.13
  104.6 3.0 collective-permute-done.13
  109.2 4.5 %collective-permute-start.14 = (f32[8,10,1]{2,1,0:T(8,128)S(1)}, f32[8,10,1]{2,1,0:T(8,128)S(1)}, u32[]{:S(2)}, u32[]{:S(2)}) collective-permute-start(f32[8,10,1]{2,1,0:T(8,128)S(1)} %get-tuple-element.264), channel_id=1, source_target_pairs={{0,1},{1,2},{2,3},{4,5},{5,6},{6,7},{8,9},{9,10},{10,11},{12,13},{... | collective-permute-start | bytes 968 | tf_op jit(solution)/shard_map/ppermute | solution.py:32
  116.5 13.0 %all-reduce.11 = (f32[]{:T(128)}, f32[]{:T(128)}) all-reduce(f32[]{:T(128)} %get-tuple-element.9, f32[]{:T(128)} %get-tuple-element.8), channel_id=1, replica_groups=mesh['gx'=8,'sp'=4] {'gx'}, use_global_device_ids=true, to_apply=%region_15.16 | all-reduce | flops 2 | bytes 16 | tf_op jit(solution)/shard_map/psum | solution.py:17
  129.5 11.1 %all-reduce.17 = (f32[]{:T(128)}, f32[]{:T(128)}) all-reduce(f32[]{:T(128)} %get-tuple-element.22, f32[]{:T(128)} %get-tuple-element.23), channel_id=1, replica_groups=mesh['gx'=8,'sp'=4] {'sp'}, use_global_device_ids=true, to_apply=%region_16.17 | all-reduce | flops 2 | bytes 16 | tf_op jit(solution)/shard_map/psum | solution.py:17
  146.5 3.6 collective-permute-start.17
  150.1 3.0 collective-permute-done.17
  154.5 4.5 %collective-permute-start.18 = (f32[8,10,1]{2,1,0:T(8,128)S(1)}, f32[8,10,1]{2,1,0:T(8,128)S(1)}, u32[]{:S(2)}, u32[]{:S(2)}) collective-permute-start(f32[8,10,1]{2,1,0:T(8,128)S(1)} %get-tuple-element.262), channel_id=1, source_target_pairs={{0,1},{1,2},{2,3},{4,5},{5,6},{6,7},{8,9},{9,10},{10,11},{12,13},{... | collective-permute-start | bytes 968 | tf_op jit(solution)/shard_map/ppermute | solution.py:32
  162.0 13.0 %all-reduce.10 = (f32[]{:T(128)}, f32[]{:T(128)}) all-reduce(f32[]{:T(128)} %get-tuple-element.7, f32[]{:T(128)} %get-tuple-element.6), channel_id=1, replica_groups=mesh['gx'=8,'sp'=4] {'gx'}, use_global_device_ids=true, to_apply=%region_21.22 | all-reduce | flops 2 | bytes 16 | tf_op jit(solution)/shard_map/psum | solution.py:17
  175.0 11.2 %all-reduce.16 = (f32[]{:T(128)}, f32[]{:T(128)}) all-reduce(f32[]{:T(128)} %get-tuple-element.20, f32[]{:T(128)} %get-tuple-element.21), channel_id=1, replica_groups=mesh['gx'=8,'sp'=4] {'sp'}, use_global_device_ids=true, to_apply=%region_22.23 | all-reduce | flops 2 | bytes 16 | tf_op jit(solution)/shard_map/psum | solution.py:17
  192.0 3.6 collective-permute-start.21
  195.7 3.0 collective-permute-done.21
  200.1 4.5 %collective-permute-start.22 = (f32[8,10,1]{2,1,0:T(8,128)S(1)}, f32[8,10,1]{2,1,0:T(8,128)S(1)}, u32[]{:S(2)}, u32[]{:S(2)}) collective-permute-start(f32[8,10,1]{2,1,0:T(8,128)S(1)} %get-tuple-element.260), channel_id=1, source_target_pairs={{0,1},{1,2},{2,3},{4,5},{5,6},{6,7},{8,9},{9,10},{10,11},{12,13},{... | collective-permute-start | bytes 968 | tf_op jit(solution)/shard_map/ppermute | solution.py:32
  207.4 13.0 %all-reduce.9 = (f32[]{:T(128)}, f32[]{:T(128)}) all-reduce(f32[]{:T(128)} %get-tuple-element.5, f32[]{:T(128)} %get-tuple-element.4), channel_id=1, replica_groups=mesh['gx'=8,'sp'=4] {'gx'}, use_global_device_ids=true, to_apply=%region_27.28 | all-reduce | flops 2 | bytes 16 | tf_op jit(solution)/shard_map/psum | solution.py:17
  220.4 11.1 %all-reduce.15 = (f32[]{:T(128)}, f32[]{:T(128)}) all-reduce(f32[]{:T(128)} %get-tuple-element.18, f32[]{:T(128)} %get-tuple-element.19), channel_id=1, replica_groups=mesh['gx'=8,'sp'=4] {'sp'}, use_global_device_ids=true, to_apply=%region_28.29 | all-reduce | flops 2 | bytes 16 | tf_op jit(solution)/shard_map/psum | solution.py:17
  238.0 3.6 collective-permute-start.25
  241.9 2.8 collective-permute-done.25
  246.1 4.5 %collective-permute-start.26 = (f32[8,10,1]{2,1,0:T(8,128)S(1)}, f32[8,10,1]{2,1,0:T(8,128)S(1)}, u32[]{:S(2)}, u32[]{:S(2)}) collective-permute-start(f32[8,10,1]{2,1,0:T(8,128)S(1)} %get-tuple-element.258), channel_id=1, source_target_pairs={{0,1},{1,2},{2,3},{4,5},{5,6},{6,7},{8,9},{9,10},{10,11},{12,13},{... | collective-permute-start | bytes 968 | tf_op jit(solution)/shard_map/ppermute | solution.py:32
  250.6 13.6 %all_gather.7 = f32[8,8,512]{2,1,0:T(8,128)S(1)} all-gather(f32[8,8,128]{2,1,0:T(8,128)S(1)} %get-tuple-element.14), channel_id=1, replica_groups=mesh['gx'=8,'sp'=4] {'sp'}, dimensions={2}, use_global_device_ids=true | all-gather | bytes 163840 | tf_op jit(solution)/shard_map/all_gather | solution.py:207
  265.2 11.8 %all-reduce.8 = (f32[]{:T(128)}, f32[]{:T(128)}) all-reduce(f32[]{:T(128)} %get-tuple-element.222, f32[]{:T(128)} %fusion.320), channel_id=1, replica_groups=mesh['gx'=8,'sp'=4] {'gx'}, use_global_device_ids=true, to_apply=%region_33.34 | all-reduce | flops 2 | bytes 16 | tf_op jit(solution)/shard_map/psum | solution.py:17
  277.1 9.0 %all-reduce.14 = (f32[]{:T(128)}, f32[]{:T(128)}) all-reduce(f32[]{:T(128)} %get-tuple-element.16, f32[]{:T(128)} %get-tuple-element.17), channel_id=1, replica_groups=mesh['gx'=8,'sp'=4] {'sp'}, use_global_device_ids=true, to_apply=%region_34.35 | all-reduce | flops 2 | bytes 16 | tf_op jit(solution)/shard_map/psum | solution.py:17
  290.1 13.4 %all_gather.6 = f32[8,8,512]{2,1,0:T(8,128)S(1)} all-gather(f32[8,8,128]{2,1,0:T(8,128)S(1)} %multiply_add_fusion), channel_id=1, replica_groups=mesh['gx'=8,'sp'=4] {'sp'}, dimensions={2}, use_global_device_ids=true | all-gather | bytes 163840 | tf_op jit(solution)/shard_map/all_gather | solution.py:206
  305.6 3.6 collective-permute-start.29
  315.1 4.1 copy.54
  319.2 6.1 %reshape.95 = f32[4,1,24576]{2,1,0:T(1,128)} reshape(f32[512,3,8,8]{3,2,1,0:T(8,128)} %bitcast.69) | data formatting | bytes 786432
  325.2 3.6 all-to-all-start
  329.4 9.3 %all-to-all-done = f32[4,1,24576]{2,1,0:T(1,128)S(1)} async-done(((f32[4,1,24576]{2,1,0:T(1,128)}), f32[4,1,24576]{2,1,0:T(1,128)S(1)}, u32[]{:S(2)}, u32[]{:S(2)}) %all-to-all-start) | async-done | bytes 393248 | tf_op jit(solution)/shard_map/all_to_all | solution.py:155
  341.0 6.2 %reshape.96 = f32[512,3,8,8]{3,2,1,0:T(8,128)} reshape(f32[4,24576]{1,0:T(4,128)S(1)} %reduce) | data formatting | bytes 786432
  347.2 4.3 %copy.55 = f32[3,8,8,4,128]{4,2,1,0,3:T(8,128)S(1)} copy(f32[3,8,8,4,128]{2,1,0,4,3:T(8,128)} %bitcast.70) | data formatting | bytes 786432 | tf_op jit(solution)/shard_map/all_to_all | solution.py:155
  352.8 3.9 convolution_multiply_fusion.1
  356.7 7.2 %subtract_multiply_fusion.64 = (f32[1,8192]{1,0:T(1,128)S(1)}, f32[1,8192]{1,0:T(1,128)S(1)}, f32[1,8192]{1,0:T(1,128)S(1)}, f32[1,8192]{1,0:T(1,128)S(1)}, f32[...) fusion(f32[12,8192]{1,0:T(8,128)S(1)} %fusion.3, ...), kind=kLoop, calls=%fused_computation.862 | loop fusion | flops 5136384 | bytes 4751360 | tf_op jit(solution)/shard_map/mul | solution.py:104
  363.9 3.0 subtract_multiply_fusion.57
  366.9 4.1 %subtract_multiply_fusion.46 = (f32[1,8192]{1,0:T(1,128)S(1)}, f32[1,8192]{1,0:T(1,128)S(1)}, f32[1,8192]{1,0:T(1,128)S(1)}, f32[1,8192]{1,0:T(1,128)S(1)}, f32[...) fusion(f32[1,8192]{1,0:T(1,128)S(1)} %get-tuple-element.221, ...), kind=kLoop, calls=%fused_computation.843 | loop fusion | flops 2220032 | bytes 3342336 | tf_op jit(solution)/shard_map/mul | solution.py:110
  372.9 3.9 convolution_multiply_fusion
  376.8 7.3 %subtract_multiply_fusion.18 = (f32[1,8192]{1,0:T(1,128)S(1)}, f32[1,8192]{1,0:T(1,128)S(1)}, f32[1,8192]{1,0:T(1,128)S(1)}, f32[1,8192]{1,0:T(1,128)S(1)}, f32[...) fusion(f32[12,8192]{1,0:T(8,128)S(1)} %fusion.1, ...), kind=kLoop, calls=%fused_computation.808 | loop fusion | flops 5136384 | bytes 4751360 | tf_op jit(solution)/shard_map/mul | solution.py:104
  384.1 2.7 subtract_multiply_fusion.11
  386.8 4.1 %subtract_multiply_fusion = (f32[1,8192]{1,0:T(1,128)S(1)}, f32[1,8192]{1,0:T(1,128)S(1)}, f32[1,8192]{1,0:T(1,128)S(1)}, f32[1,8192]{1,0:T(1,128)S(1)}, f32[1,8...) fusion(f32[1,8192]{1,0:T(1,128)S(1)} %get-tuple-element.130, ...), kind=kLoop, calls=%fused_computation.789 | loop fusion | flops 2220032 | bytes 3342336 | tf_op jit(solution)/shard_map/mul | solution.py:110
  391.3 17.4 %all_to_all.33 = f32[12,8,8,128]{3,2,1,0:T(8,128)S(1)} all-to-all(f32[12,8,8,128]{3,2,1,0:T(8,128)S(1)} %fusion.11), channel_id=1, replica_groups=mesh['gx'=8,'sp'=4] {'sp'}, dimensions={0} | all-to-all | bytes 786432 | tf_op jit(solution)/shard_map/all_to_all | solution.py:219
  (143 shorter events, 57.9 us)
Async XLA Ops:
  1.5 11.0 %collective-permute-start.1 = (f32[8,1,128]{2,1,0:T(1,128)S(1)}, f32[8,1,128]{2,1,0:T(1,128)S(1)}, u32[]{:S(2)}, u32[]{:S(2)}) collective-permute-start(f32[8,1,128]{2,1,0:T(1,128)S(1)} %get-tuple-element.281), channel_id=1, source_target_pairs={{4,0},{8,4},{12,8},{16,12},{20,16},{24,20},{28,24},{5,1},{9,5},{13... | collective-permute-start | bytes 12296 | tf_op jit(solution)/shard_map/ppermute | solution.py:34
  3.5 9.0 %collective-permute-start = (f32[8,1,128]{2,1,0:T(1,128)S(1)}, f32[8,1,128]{2,1,0:T(1,128)S(1)}, u32[]{:S(2)}, u32[]{:S(2)}) collective-permute-start(f32[8,1,128]{2,1,0:T(1,128)S(1)} %get-tuple-element.282), channel_id=1, source_target_pairs={{0,4},{4,8},{8,12},{12,16},{16,20},{20,24},{24,28},{1,5},{5,9},{9,... | collective-permute-start | bytes 12296 | tf_op jit(solution)/shard_map/ppermute | solution.py:32
  6.7 10.7 %collective-permute-start.4 = (f32[8,1,128]{2,1,0:T(1,128)S(1)}, f32[8,1,128]{2,1,0:T(1,128)S(1)}, u32[]{:S(2)}, u32[]{:S(2)}) collective-permute-start(f32[8,1,128]{2,1,0:T(1,128)S(1)} %get-tuple-element.283), channel_id=1, source_target_pairs={{0,4},{4,8},{8,12},{12,16},{16,20},{20,24},{24,28},{1,5},{5,9},{9,... | collective-permute-start | bytes 12296 | tf_op jit(solution)/shard_map/ppermute | solution.py:32
  10.5 6.9 %collective-permute-start.5 = (f32[8,1,128]{2,1,0:T(1,128)S(1)}, f32[8,1,128]{2,1,0:T(1,128)S(1)}, u32[]{:S(2)}, u32[]{:S(2)}) collective-permute-start(f32[8,1,128]{2,1,0:T(1,128)S(1)} %get-tuple-element.284), channel_id=1, source_target_pairs={{4,0},{8,4},{12,8},{16,12},{20,16},{24,20},{28,24},{5,1},{9,5},{13... | collective-permute-start | bytes 12296 | tf_op jit(solution)/shard_map/ppermute | solution.py:34
  12.6 11.4 %collective-permute-start.2 = (f32[8,10,1]{2,1,0:T(8,128)S(1)}, f32[8,10,1]{2,1,0:T(8,128)S(1)}, u32[]{:S(2)}, u32[]{:S(2)}) collective-permute-start(f32[8,10,1]{2,1,0:T(8,128)S(1)} %get-tuple-element.267), channel_id=1, source_target_pairs={{0,1},{1,2},{2,3},{4,5},{5,6},{6,7},{8,9},{9,10},{10,11},{12,13},{... | collective-permute-start | bytes 968 | tf_op jit(solution)/shard_map/ppermute | solution.py:32
  16.1 7.9 %collective-permute-start.3 = (f32[8,10,1]{2,1,0:T(8,128)S(1)}, f32[8,10,1]{2,1,0:T(8,128)S(1)}, u32[]{:S(2)}, u32[]{:S(2)}) collective-permute-start(f32[8,10,1]{2,1,0:T(8,128)S(1)} %get-tuple-element.268), channel_id=1, source_target_pairs={{1,0},{2,1},{3,2},{5,4},{6,5},{7,6},{9,8},{10,9},{11,10},{13,12},{... | collective-permute-start | bytes 968 | tf_op jit(solution)/shard_map/ppermute | solution.py:34
  17.5 6.8 %collective-permute-start.7 = (f32[8,10,1]{2,1,0:T(8,128)S(1)}, f32[8,10,1]{2,1,0:T(8,128)S(1)}, u32[]{:S(2)}, u32[]{:S(2)}) collective-permute-start(f32[8,10,1]{2,1,0:T(8,128)S(1)} %get-tuple-element.269), channel_id=1, source_target_pairs={{1,0},{2,1},{3,2},{5,4},{6,5},{7,6},{9,8},{10,9},{11,10},{13,12},{... | collective-permute-start | bytes 968 | tf_op jit(solution)/shard_map/ppermute | solution.py:34
  18.8 7.1 %collective-permute-start.6 = (f32[8,10,1]{2,1,0:T(8,128)S(1)}, f32[8,10,1]{2,1,0:T(8,128)S(1)}, u32[]{:S(2)}, u32[]{:S(2)}) collective-permute-start(f32[8,10,1]{2,1,0:T(8,128)S(1)} %get-tuple-element.270), channel_id=1, source_target_pairs={{0,1},{1,2},{2,3},{4,5},{5,6},{6,7},{8,9},{9,10},{10,11},{12,13},{... | collective-permute-start | bytes 968 | tf_op jit(solution)/shard_map/ppermute | solution.py:32
  53.3 5.6 %collective-permute-start.8 = (f32[8,1,128]{2,1,0:T(1,128)S(1)}, f32[8,1,128]{2,1,0:T(1,128)S(1)}, u32[]{:S(2)}, u32[]{:S(2)}) collective-permute-start(f32[8,1,128]{2,1,0:T(1,128)S(1)} %get-tuple-element.279), channel_id=1, source_target_pairs={{0,4},{4,8},{8,12},{12,16},{16,20},{20,24},{24,28},{1,5},{5,9},{9,... | collective-permute-start | bytes 12296 | tf_op jit(solution)/shard_map/ppermute | solution.py:32
  55.3 6.3 %collective-permute-start.9 = (f32[8,1,128]{2,1,0:T(1,128)S(1)}, f32[8,1,128]{2,1,0:T(1,128)S(1)}, u32[]{:S(2)}, u32[]{:S(2)}) collective-permute-start(f32[8,1,128]{2,1,0:T(1,128)S(1)} %get-tuple-element.280), channel_id=1, source_target_pairs={{4,0},{8,4},{12,8},{16,12},{20,16},{24,20},{28,24},{5,1},{9,5},{13... | collective-permute-start | bytes 12296 | tf_op jit(solution)/shard_map/ppermute | solution.py:34
  61.7 6.2 %collective-permute-start.11 = (f32[8,10,1]{2,1,0:T(8,128)S(1)}, f32[8,10,1]{2,1,0:T(8,128)S(1)}, u32[]{:S(2)}, u32[]{:S(2)}) collective-permute-start(f32[8,10,1]{2,1,0:T(8,128)S(1)} %get-tuple-element.265), channel_id=1, source_target_pairs={{1,0},{2,1},{3,2},{5,4},{6,5},{7,6},{9,8},{10,9},{11,10},{13,12},{... | collective-permute-start | bytes 968 | tf_op jit(solution)/shard_map/ppermute | solution.py:34
  63.0 6.4 %collective-permute-start.10 = (f32[8,10,1]{2,1,0:T(8,128)S(1)}, f32[8,10,1]{2,1,0:T(8,128)S(1)}, u32[]{:S(2)}, u32[]{:S(2)}) collective-permute-start(f32[8,10,1]{2,1,0:T(8,128)S(1)} %get-tuple-element.266), channel_id=1, source_target_pairs={{0,1},{1,2},{2,3},{4,5},{5,6},{6,7},{8,9},{9,10},{10,11},{12,13},{... | collective-permute-start | bytes 968 | tf_op jit(solution)/shard_map/ppermute | solution.py:32
  99.1 5.6 %collective-permute-start.12 = (f32[8,1,128]{2,1,0:T(1,128)S(1)}, f32[8,1,128]{2,1,0:T(1,128)S(1)}, u32[]{:S(2)}, u32[]{:S(2)}) collective-permute-start(f32[8,1,128]{2,1,0:T(1,128)S(1)} %get-tuple-element.277), channel_id=1, source_target_pairs={{0,4},{4,8},{8,12},{12,16},{16,20},{20,24},{24,28},{1,5},{5,9},{9,... | collective-permute-start | bytes 12296 | tf_op jit(solution)/shard_map/ppermute | solution.py:32
  101.0 6.7 %collective-permute-start.13 = (f32[8,1,128]{2,1,0:T(1,128)S(1)}, f32[8,1,128]{2,1,0:T(1,128)S(1)}, u32[]{:S(2)}, u32[]{:S(2)}) collective-permute-start(f32[8,1,128]{2,1,0:T(1,128)S(1)} %get-tuple-element.278), channel_id=1, source_target_pairs={{4,0},{8,4},{12,8},{16,12},{20,16},{24,20},{28,24},{5,1},{9,5},{13... | collective-permute-start | bytes 12296 | tf_op jit(solution)/shard_map/ppermute | solution.py:34
  107.7 134.0 %copy-start = (f32[3,8,8,512]{3,2,1,0:T(8,128)S(1)}, f32[3,8,8,512]{3,2,1,0:T(8,128)}, u32[]{:S(2)}) copy-start(f32[3,8,8,512]{3,2,1,0:T(8,128)} %param.15) | copy-start | bytes 1179652
  107.8 6.3 %collective-permute-start.15 = (f32[8,10,1]{2,1,0:T(8,128)S(1)}, f32[8,10,1]{2,1,0:T(8,128)S(1)}, u32[]{:S(2)}, u32[]{:S(2)}) collective-permute-start(f32[8,10,1]{2,1,0:T(8,128)S(1)} %get-tuple-element.263), channel_id=1, source_target_pairs={{1,0},{2,1},{3,2},{5,4},{6,5},{7,6},{9,8},{10,9},{11,10},{13,12},{... | collective-permute-start | bytes 968 | tf_op jit(solution)/shard_map/ppermute | solution.py:34
  109.2 6.4 %collective-permute-start.14 = (f32[8,10,1]{2,1,0:T(8,128)S(1)}, f32[8,10,1]{2,1,0:T(8,128)S(1)}, u32[]{:S(2)}, u32[]{:S(2)}) collective-permute-start(f32[8,10,1]{2,1,0:T(8,128)S(1)} %get-tuple-element.264), channel_id=1, source_target_pairs={{0,1},{1,2},{2,3},{4,5},{5,6},{6,7},{8,9},{9,10},{10,11},{12,13},{... | collective-permute-start | bytes 968 | tf_op jit(solution)/shard_map/ppermute | solution.py:32
  144.6 5.6 %collective-permute-start.16 = (f32[8,1,128]{2,1,0:T(1,128)S(1)}, f32[8,1,128]{2,1,0:T(1,128)S(1)}, u32[]{:S(2)}, u32[]{:S(2)}) collective-permute-start(f32[8,1,128]{2,1,0:T(1,128)S(1)} %get-tuple-element.275), channel_id=1, source_target_pairs={{0,4},{4,8},{8,12},{12,16},{16,20},{20,24},{24,28},{1,5},{5,9},{9,... | collective-permute-start | bytes 12296 | tf_op jit(solution)/shard_map/ppermute | solution.py:32
  146.5 6.7 %collective-permute-start.17 = (f32[8,1,128]{2,1,0:T(1,128)S(1)}, f32[8,1,128]{2,1,0:T(1,128)S(1)}, u32[]{:S(2)}, u32[]{:S(2)}) collective-permute-start(f32[8,1,128]{2,1,0:T(1,128)S(1)} %get-tuple-element.276), channel_id=1, source_target_pairs={{4,0},{8,4},{12,8},{16,12},{20,16},{24,20},{28,24},{5,1},{9,5},{13... | collective-permute-start | bytes 12296 | tf_op jit(solution)/shard_map/ppermute | solution.py:34
  153.3 6.2 %collective-permute-start.19 = (f32[8,10,1]{2,1,0:T(8,128)S(1)}, f32[8,10,1]{2,1,0:T(8,128)S(1)}, u32[]{:S(2)}, u32[]{:S(2)}) collective-permute-start(f32[8,10,1]{2,1,0:T(8,128)S(1)} %get-tuple-element.261), channel_id=1, source_target_pairs={{1,0},{2,1},{3,2},{5,4},{6,5},{7,6},{9,8},{10,9},{11,10},{13,12},{... | collective-permute-start | bytes 968 | tf_op jit(solution)/shard_map/ppermute | solution.py:34
  154.5 6.4 %collective-permute-start.18 = (f32[8,10,1]{2,1,0:T(8,128)S(1)}, f32[8,10,1]{2,1,0:T(8,128)S(1)}, u32[]{:S(2)}, u32[]{:S(2)}) collective-permute-start(f32[8,10,1]{2,1,0:T(8,128)S(1)} %get-tuple-element.262), channel_id=1, source_target_pairs={{0,1},{1,2},{2,3},{4,5},{5,6},{6,7},{8,9},{9,10},{10,11},{12,13},{... | collective-permute-start | bytes 968 | tf_op jit(solution)/shard_map/ppermute | solution.py:32
  190.1 5.6 %collective-permute-start.20 = (f32[8,1,128]{2,1,0:T(1,128)S(1)}, f32[8,1,128]{2,1,0:T(1,128)S(1)}, u32[]{:S(2)}, u32[]{:S(2)}) collective-permute-start(f32[8,1,128]{2,1,0:T(1,128)S(1)} %get-tuple-element.273), channel_id=1, source_target_pairs={{0,4},{4,8},{8,12},{12,16},{16,20},{20,24},{24,28},{1,5},{5,9},{9,... | collective-permute-start | bytes 12296 | tf_op jit(solution)/shard_map/ppermute | solution.py:32
  192.0 6.7 %collective-permute-start.21 = (f32[8,1,128]{2,1,0:T(1,128)S(1)}, f32[8,1,128]{2,1,0:T(1,128)S(1)}, u32[]{:S(2)}, u32[]{:S(2)}) collective-permute-start(f32[8,1,128]{2,1,0:T(1,128)S(1)} %get-tuple-element.274), channel_id=1, source_target_pairs={{4,0},{8,4},{12,8},{16,12},{20,16},{24,20},{28,24},{5,1},{9,5},{13... | collective-permute-start | bytes 12296 | tf_op jit(solution)/shard_map/ppermute | solution.py:34
  198.8 6.2 %collective-permute-start.23 = (f32[8,10,1]{2,1,0:T(8,128)S(1)}, f32[8,10,1]{2,1,0:T(8,128)S(1)}, u32[]{:S(2)}, u32[]{:S(2)}) collective-permute-start(f32[8,10,1]{2,1,0:T(8,128)S(1)} %get-tuple-element.259), channel_id=1, source_target_pairs={{1,0},{2,1},{3,2},{5,4},{6,5},{7,6},{9,8},{10,9},{11,10},{13,12},{... | collective-permute-start | bytes 968 | tf_op jit(solution)/shard_map/ppermute | solution.py:34
  200.1 6.4 %collective-permute-start.22 = (f32[8,10,1]{2,1,0:T(8,128)S(1)}, f32[8,10,1]{2,1,0:T(8,128)S(1)}, u32[]{:S(2)}, u32[]{:S(2)}) collective-permute-start(f32[8,10,1]{2,1,0:T(8,128)S(1)} %get-tuple-element.260), channel_id=1, source_target_pairs={{0,1},{1,2},{2,3},{4,5},{5,6},{6,7},{8,9},{9,10},{10,11},{12,13},{... | collective-permute-start | bytes 968 | tf_op jit(solution)/shard_map/ppermute | solution.py:32
  236.1 5.8 %collective-permute-start.24 = (f32[8,1,128]{2,1,0:T(1,128)S(1)}, f32[8,1,128]{2,1,0:T(1,128)S(1)}, u32[]{:S(2)}, u32[]{:S(2)}) collective-permute-start(f32[8,1,128]{2,1,0:T(1,128)S(1)} %get-tuple-element.271), channel_id=1, source_target_pairs={{0,4},{4,8},{8,12},{12,16},{16,20},{20,24},{24,28},{1,5},{5,9},{9,... | collective-permute-start | bytes 12296 | tf_op jit(solution)/shard_map/ppermute | solution.py:32
  238.0 6.7 %collective-permute-start.25 = (f32[8,1,128]{2,1,0:T(1,128)S(1)}, f32[8,1,128]{2,1,0:T(1,128)S(1)}, u32[]{:S(2)}, u32[]{:S(2)}) collective-permute-start(f32[8,1,128]{2,1,0:T(1,128)S(1)} %get-tuple-element.272), channel_id=1, source_target_pairs={{4,0},{8,4},{12,8},{16,12},{20,16},{24,20},{28,24},{5,1},{9,5},{13... | collective-permute-start | bytes 12296 | tf_op jit(solution)/shard_map/ppermute | solution.py:34
  244.8 19.5 %collective-permute-start.27 = (f32[8,10,1]{2,1,0:T(8,128)S(1)}, f32[8,10,1]{2,1,0:T(8,128)S(1)}, u32[]{:S(2)}, u32[]{:S(2)}) collective-permute-start(f32[8,10,1]{2,1,0:T(8,128)S(1)} %get-tuple-element.257), channel_id=1, source_target_pairs={{1,0},{2,1},{3,2},{5,4},{6,5},{7,6},{9,8},{10,9},{11,10},{13,12},{... | collective-permute-start | bytes 968 | tf_op jit(solution)/shard_map/ppermute | solution.py:34
  246.1 18.2 %collective-permute-start.26 = (f32[8,10,1]{2,1,0:T(8,128)S(1)}, f32[8,10,1]{2,1,0:T(8,128)S(1)}, u32[]{:S(2)}, u32[]{:S(2)}) collective-permute-start(f32[8,10,1]{2,1,0:T(8,128)S(1)} %get-tuple-element.258), channel_id=1, source_target_pairs={{0,1},{1,2},{2,3},{4,5},{5,6},{6,7},{8,9},{9,10},{10,11},{12,13},{... | collective-permute-start | bytes 968 | tf_op jit(solution)/shard_map/ppermute | solution.py:32
  290.1 22.6 %copy-start.2 = (f32[8,8,128]{2,1,0:T(8,128)}, f32[8,8,128]{2,1,0:T(8,128)S(1)}, u32[]{:S(2)}) copy-start(f32[8,8,128]{2,1,0:T(8,128)S(1)} %multiply_add_fusion) | copy-start | bytes 98308
  303.7 5.8 %collective-permute-start.28 = (f32[5,8,1,512]{3,1,2,0:T(8,128)S(1)}, f32[5,8,1,512]{3,1,2,0:T(8,128)S(1)}, u32[]{:S(2)}, u32[]{:S(2)}) collective-permute-start(f32[5,8,1,512]{3,1,2,0:T(8,128)S(1)} %get-tuple-element.249), channel_id=1, source_target_pairs={{0,4},{4,8},{8,12},{12,16},{16,20},{20,24},{24,28},{1,5},{5,9},{9,... | collective-permute-start | bytes 245768 | tf_op jit(solution)/shard_map/ppermute | solution.py:32
  305.6 6.4 %collective-permute-start.29 = (f32[5,8,1,512]{3,1,2,0:T(8,128)S(1)}, f32[5,8,1,512]{3,1,2,0:T(8,128)S(1)}, u32[]{:S(2)}, u32[]{:S(2)}) collective-permute-start(f32[5,8,1,512]{3,1,2,0:T(8,128)S(1)} %get-tuple-element.250), channel_id=1, source_target_pairs={{4,0},{8,4},{12,8},{16,12},{20,16},{24,20},{28,24},{5,1},{9,5},{13... | collective-permute-start | bytes 245768 | tf_op jit(solution)/shard_map/ppermute | solution.py:34
  319.2 9.7 %copy-start.3 = (s32[8,8,128]{2,1,0:T(8,128)S(1)}, s32[8,8,128]{2,1,0:T(8,128)}, u32[]{:S(2)}) copy-start(s32[8,8,128]{2,1,0:T(8,128)} %param.16) | copy-start | bytes 98308
  319.2 9.8 %copy-start.1 = (f32[12,8]{0,1:T(8,128)S(1)}, f32[12,8]{0,1:T(8,128)}, u32[]{:S(2)}) copy-start(f32[12,8]{0,1:T(8,128)} %param.18) | copy-start | bytes 1156
  319.2 10.0 %copy-start.4 = (f32[6,8]{1,0:T(8,128)S(1)}, f32[6,8]{1,0:T(8,128)}, u32[]{:S(2)}) copy-start(f32[6,8]{1,0:T(8,128)} %param.17) | copy-start | bytes 580
  325.2 13.5 %all-to-all-start = ((f32[4,1,24576]{2,1,0:T(1,128)}), f32[4,1,24576]{2,1,0:T(1,128)S(1)}, u32[]{:S(2)}, u32[]{:S(2)}) async-start(f32[4,1,24576]{2,1,0:T(1,128)} %reshape.95), calls=%async_computation | async-start | bytes 786432 | tf_op jit(solution)/shard_map/all_to_all | solution.py:155
  347.2 4.4 %copy-start.5 = (f32[8]{0:T(128)S(1)}, f32[8]{0:T(128)}, u32[]{:S(2)}) copy-start(f32[8]{0:T(128)} %param.19) | copy-start | bytes 100
